TPU v7x, 32 devices: a whole 2x2x4 slice. The times are simulated.
32 devices in a mesh: groups: 2 (over x), row: 16 (over z, y, core).
Axes of the slice: x: 2, y: 2, z: 4, core: 2. Of those that a mesh axis runs over, the one named last changes fastest.
Arguments:
- factor_panel: bfloat16 [32768, 2048], P(('groups', 'row')), parts along dimension 0, may hold values from -0.25 to 0.25
- pivots: float32 [4096], P('groups'), parts along dimension 0, may hold values from 1 to 1.25
- right_sides: float32 [32768, 256], P(('groups', 'row')), parts along dimension 0, may hold values from -6 to 6
- block_home: int32 [32], replicated, may hold values from 0 to 31, each once
Outputs:
- remainder: float32 [32768, 256], P('groups', 'row'), parts along dimension 0
- psf_variance: float32 [512], P(('groups', 'row')), parts along dimension 0
There are 2 independent parts, one for each index of `groups`. A program takes and returns all parts, laid end to end along the dimension named above; an argument that names none is the same for every part. Nothing has to cross between parts.
Inputs may be any that keep to these rules, and one draw needn't show every extreme that they name: block_home[g] is the stored position of global block g; position p is slot p % 2 of row device p // 2; every position holds exactly one block.
All inputs are finite; a program needn't handle non-finite values.
Results may differ from a plain program's by a relative error of at most 0.0042.
Values may be sent and summed in bfloat16 or wider, within the bound.
No kernel may reach another device: no remote copies, remote signals or barrier semaphores. Data moves between devices by JAX's collectives and lax.ppermute only.
A program may use at most 128 MiB of HBM per device.

v0:
```python
import jax
import jax.numpy as jnp
from jax import lax
from jax.sharding import PartitionSpec as P

BLOCK = 512
STEPS = 4
PANEL = 2048


def spread(value, axis, source):
    kept = jnp.where(lax.axis_index(axis) == source, value, 0).astype(value.dtype)
    return lax.psum(kept, axis)


def on_device(factor_panel, pivots, right_sides, block_home):
    slot_count = factor_panel.shape[0] // BLOCK
    columns_all = right_sides.shape[1]
    row_count = lax.axis_size("row")
    row_index = lax.axis_index("row")
    block_total = block_home.shape[0]
    positions = row_index * slot_count + jnp.arange(slot_count, dtype=jnp.int32)
    global_ids = jnp.sum(
        jnp.where(
            block_home[None, :] == positions[:, None],
            jnp.arange(block_total, dtype=jnp.int32)[None, :],
            0,
        ),
        axis=1,
    )
    partial_value = right_sides.reshape(slot_count, BLOCK, columns_all)
    factor_blocks = factor_panel.reshape(slot_count, BLOCK, PANEL)
    my_columns = columns_all // row_count
    solutions = []
    for k in range(STEPS):
        slot = block_home[k] % slot_count
        rows = lax.dynamic_index_in_dim(partial_value, slot, 0, keepdims=False)
        diag_slot = block_home[k] % slot_count
        held = lax.dynamic_index_in_dim(factor_blocks, diag_slot, 0, keepdims=False)
        diag_rows = held[:, k * BLOCK : (k + 1) * BLOCK].astype(jnp.float32)
        diag_block = jnp.tril(diag_rows, -1) + jnp.diag(pivots[k * BLOCK : (k + 1) * BLOCK])
        solution = jax.scipy.linalg.solve_triangular(diag_block, rows, lower=True).astype(
            jnp.bfloat16
        )
        solution = spread(solution, "row", block_home[k] // slot_count)
        active = (global_ids > k).astype(jnp.float32)
        product = jnp.einsum(
            "sij,jc->sic",
            factor_blocks[:, :, k * BLOCK : (k + 1) * BLOCK],
            solution,
            preferred_element_type=jnp.float32,
        )
        partial_value = partial_value - active[:, None, None] * product
        partial_value = jnp.where(
            (global_ids == k)[:, None, None], solution.astype(jnp.float32)[None], partial_value
        )
        solutions.append(solution)
    stored = lax.all_to_all(
        partial_value.reshape(slot_count * BLOCK, columns_all),
        "row",
        split_axis=1,
        concat_axis=0,
        tiled=True,
    )
    ordered = jnp.take(stored.reshape(block_total, BLOCK, my_columns), block_home, axis=0)
    remainder = ordered.reshape(block_total * BLOCK, my_columns)
    solved = remainder[: STEPS * BLOCK]
    psf_variance = jnp.mean(solved * solved, axis=0)
    return (remainder, psf_variance)


def solution(mesh):
    in_specs = (P(("groups", "row"), None), P("groups"), P(("groups", "row"), None), P())
    out_specs = (P("groups", "row"), P(("groups", "row")))
    return jax.shard_map(
        on_device, mesh=mesh, in_specs=in_specs, out_specs=out_specs, check_vma=False
    )
```

profile of v0, /device:TPU:9, one launch (start us, length us, event | category | flops | bytes accessed | tf_op | source)
XLA Modules:
  0.0 519.9 jit_solution(8942205453289188810)
XLA Ops:
  7.2 1.4 fusion.108
  17.5 4.6 dynamic-slice_bitcast_fusion.3
  22.1 2.0 fusion.19
  24.1 12.0 %while.8 = (s32[]{:T(128)}, f32[512,512]{1,0:T(8,128)}, s32[4,2]{0,1:T(2,128)S(1)}, f32[4,128,128]{2,1,0:T(8,128)S(1)}, s32[]{:T(128)}) while((s32[]{:T(128)}, f32[512,512]{1,0:T(8,128)}, s32[4,2]{0,1:T(2,128)S(1)}, f32[4,128,128]{2,1,0:T(8,128)S(1)}, s32[]{:T(128)}) %tuple.86), condition=%wide.while_cond, body=%wide.while_body.sunk | while | flops 2 | bytes 131181 | solution.py:42
  24.8 2.3 bitcast_dynamic-update-slice_fusion.8
  27.8 2.3 bitcast_dynamic-update-slice_fusion.8
  30.8 2.3 bitcast_dynamic-update-slice_fusion.8
  33.8 2.2 bitcast_dynamic-update-slice_fusion.8
  36.8 40.1 %custom-call.6 = f32[4,128,128]{1,2,0:T(8,128)S(1)} custom-call(f32[4,128,128]{2,1,0:T(8,128)} %copy-done.2), custom_call_target="InvertDiagBlocksLowerTriangular" | custom-call | tf_op jit(solution)/shard_map/jit(_solve_triangular)/triangular_solve | solution.py:42
  78.8 1.2 convolution_subtract_fusion.7
  80.3 1.3 convolution_subtract_fusion.6
  82.8 1.6 copy.57
  85.1 7.6 %while.9 = (s32[]{:T(128)}, f32[512,512]{1,0:T(8,128)S(1)}, s32[4,2]{0,1:T(2,128)S(1)}, f32[4,128,128]{2,1,0:T(8,128)S(1)}, s32[]{:T(128)}) while((s32[]{:T(128)}, f32[512,512]{1,0:T(8,128)S(1)}, s32[4,2]{0,1:T(2,128)S(1)}, f32[4,128,128]{2,1,0:T(8,128)S(1)}, s32[]{:T(128)}) %tuple.106), condition=%wide.while_cond.clone, body=%wide.while_body.clone.sunk | while | flops 2 | bytes 131181 | solution.py:42
  85.8 1.3 bitcast_dynamic-update-slice_fusion.9
  87.7 1.3 bitcast_dynamic-update-slice_fusion.9
  89.6 1.3 bitcast_dynamic-update-slice_fusion.9
  91.5 1.3 bitcast_dynamic-update-slice_fusion.9
  93.4 40.2 %custom-call.7 = f32[4,128,128]{1,2,0:T(8,128)S(1)} custom-call(f32[4,128,128]{2,1,0:T(8,128)} %copy-done.3), custom_call_target="InvertDiagBlocksLowerTriangular" | custom-call | tf_op jit(solution)/shard_map/jit(_solve_triangular)/triangular_solve | solution.py:42
  133.7 40.1 %all-reduce.5.cloned.1.call-done = bf16[512,256]{1,0:T(8,128)(2,1)} async-done(((bf16[512,256]{1,0:T(8,128)(2,1)}), bf16[512,256]{1,0:T(8,128)(2,1)}) %all-reduce.5.cloned.1.call-update) | async-done | bytes 262160 | tf_op jit(solution)/shard_map/psum | solution.py:13
  173.7 1.9 copy.55
  175.7 1.9 fusion.11
  179.6 1.2 convolution_subtract_fusion.5
  181.1 1.3 convolution_subtract_fusion.4
  183.8 11.1 %while.10 = (s32[]{:T(128)}, f32[512,512]{1,0:T(8,128)}, s32[4,2]{0,1:T(2,128)S(1)}, f32[4,128,128]{2,1,0:T(8,128)S(1)}, s32[]{:T(128)}) while((s32[]{:T(128)}, f32[512,512]{1,0:T(8,128)}, s32[4,2]{0,1:T(2,128)S(1)}, f32[4,128,128]{2,1,0:T(8,128)S(1)}, s32[]{:T(128)}) %tuple.107), condition=%wide.while_cond.clone.1, body=%wide.while_body.clone.1.sunk | while | flops 2 | bytes 131181 | solution.py:42
  184.4 2.2 bitcast_dynamic-update-slice_fusion.10
  187.2 2.2 bitcast_dynamic-update-slice_fusion.10
  190.0 2.2 bitcast_dynamic-update-slice_fusion.10
  192.8 2.1 bitcast_dynamic-update-slice_fusion.10
  195.5 39.3 %custom-call.8 = f32[4,128,128]{1,2,0:T(8,128)S(1)} custom-call(f32[4,128,128]{2,1,0:T(8,128)S(1)} %get-tuple-element.31), custom_call_target="InvertDiagBlocksLowerTriangular" | custom-call | tf_op jit(solution)/shard_map/jit(_solve_triangular)/triangular_solve | solution.py:42
  234.9 39.7 %all-reduce.7.cloned.1.call-done = bf16[512,256]{1,0:T(8,128)(2,1)} async-done(((bf16[512,256]{1,0:T(8,128)(2,1)}), bf16[512,256]{1,0:T(8,128)(2,1)}) %all-reduce.7.cloned.1.call-update) | async-done | bytes 262160 | tf_op jit(solution)/shard_map/psum | solution.py:13
  274.6 1.9 copy.59
  276.4 1.9 fusion.8
  280.4 1.2 convolution_subtract_fusion.3
  281.9 1.3 convolution_subtract_fusion.2
  284.4 8.3 %while.11 = (s32[]{:T(128)}, f32[512,512]{1,0:T(8,128)S(1)}, s32[4,2]{0,1:T(2,128)S(1)}, f32[4,128,128]{2,1,0:T(8,128)S(1)}, s32[]{:T(128)}) while((s32[]{:T(128)}, f32[512,512]{1,0:T(8,128)S(1)}, s32[4,2]{0,1:T(2,128)S(1)}, f32[4,128,128]{2,1,0:T(8,128)S(1)}, s32[]{:T(128)}) %tuple.108), condition=%wide.while_cond.clone.2, body=%wide.while_body.clone.2.sunk | while | flops 2 | bytes 131181 | solution.py:42
  285.1 1.4 bitcast_dynamic-update-slice_fusion.11
  287.1 1.4 bitcast_dynamic-update-slice_fusion.11
  289.2 1.4 bitcast_dynamic-update-slice_fusion.11
  291.3 1.4 bitcast_dynamic-update-slice_fusion.11
  293.4 39.3 %custom-call.9 = f32[4,128,128]{1,2,0:T(8,128)S(1)} custom-call(f32[4,128,128]{2,1,0:T(8,128)S(1)} %get-tuple-element.32), custom_call_target="InvertDiagBlocksLowerTriangular" | custom-call | tf_op jit(solution)/shard_map/jit(_solve_triangular)/triangular_solve | solution.py:42
  332.7 42.4 %all-reduce.9.cloned.1.call-done = bf16[512,256]{1,0:T(8,128)(2,1)} async-done(((bf16[512,256]{1,0:T(8,128)(2,1)}), bf16[512,256]{1,0:T(8,128)(2,1)}) %all-reduce.9.cloned.1.call-update) | async-done | bytes 262160 | tf_op jit(solution)/shard_map/psum | solution.py:13
  375.1 1.9 copy.62
  377.0 1.9 fusion.5
  382.2 90.3 %all-reduce.11.cloned.1.call-done = bf16[512,256]{1,0:T(8,128)(2,1)} async-done(((bf16[512,256]{1,0:T(8,128)(2,1)}), bf16[512,256]{1,0:T(8,128)(2,1)}) %all-reduce.11.cloned.1.call-update) | async-done | bytes 262160 | tf_op jit(solution)/shard_map/psum | solution.py:13
  473.6 1.8 fusion.2
  476.2 1.9 all_to_all.12
  478.1 6.5 %all-to-all-start = ((f32[1024,16,16]{0,2,1:T(8,128)}), f32[1024,16,16]{0,2,1:T(8,128)S(1)}, u32[]{:S(2)}, u32[]{:S(2)}) async-start(f32[1024,16,16]{0,2,1:T(8,128)} %all_to_all.12), calls=%async_computation | async-start | bytes 2097152 | tf_op jit(solution)/shard_map/all_to_all | solution.py:58
  484.7 24.8 %all-to-all-done = f32[1024,16,16]{0,2,1:T(8,128)S(1)} async-done(((f32[1024,16,16]{0,2,1:T(8,128)}), f32[1024,16,16]{0,2,1:T(8,128)S(1)}, u32[]{:S(2)}, u32[]{:S(2)}) %all-to-all-start) | async-done | bytes 1048608 | tf_op jit(solution)/shard_map/all_to_all | solution.py:58
  (109 shorter events, 32.0 us)
Async XLA Ops:
  7.2 166.6 %all-reduce.5.cloned.1.call-start = ((), (), s32[]{:S(2)}) async-start(), calls=%async_computation.1 | async-start | bytes 524288 | tf_op jit(solution)/shard_map/psum | solution.py:13
  22.1 54.9 %copy-start.1 = (f32[1024,256]{1,0:T(8,128)S(1)}, f32[1024,256]{1,0:T(8,128)}, u32[]{:S(2)}) copy-start(f32[1024,256]{1,0:T(8,128)} %param.8) | copy-start | bytes 3145732
  24.1 60.8 %copy-start.4 = (s32[32]{0:T(128)S(1)}, s32[32]{0:T(128)}, u32[]{:S(2)}) copy-start(s32[32]{0:T(128)} %param.9) | copy-start | bytes 388
  36.1 0.7 copy-start.2
  82.7 191.8 %all-reduce.7.cloned.1.call-start = ((), (), s32[]{:S(2)}) async-start(), calls=%async_computation.2 | async-start | bytes 524288 | tf_op jit(solution)/shard_map/psum | solution.py:13
  92.7 0.7 copy-start.3
  93.4 82.2 %copy-start = (f32[512,512]{1,0:T(8,128)}, f32[512,512]{1,0:T(8,128)S(1)}, u32[]{:S(2)}) copy-start(f32[512,512]{1,0:T(8,128)S(1)} %get-tuple-element.280) | copy-start | bytes 3145732
  183.5 191.6 %all-reduce.9.cloned.1.call-start = ((), (), s32[]{:S(2)}) async-start(), calls=%async_computation.3 | async-start | bytes 524288 | tf_op jit(solution)/shard_map/psum | solution.py:13
  284.3 188.2 %all-reduce.11.cloned.1.call-start = ((), (), s32[]{:S(2)}) async-start(), calls=%async_computation.4 | async-start | bytes 524288 | tf_op jit(solution)/shard_map/psum | solution.py:13
  478.1 31.4 %all-to-all-start = ((f32[1024,16,16]{0,2,1:T(8,128)}), f32[1024,16,16]{0,2,1:T(8,128)S(1)}, u32[]{:S(2)}, u32[]{:S(2)}) async-start(f32[1024,16,16]{0,2,1:T(8,128)} %all_to_all.12), calls=%async_computation | async-start | bytes 2097152 | tf_op jit(solution)/shard_map/all_to_all | solution.py:58
Sparse Core Ops, SparseCore 0:
  82.8 90.8 all-reduce.4
  183.6 90.8 all-reduce.6
  284.4 90.6 all-reduce.8
  382.3 90.1 all-reduce.10
where the time goes:
time: 521 us; the launch traced here: 520 us
  waiting for transfers between devices  237 us (45%)
  other arithmetic  166 us (32%)
  local copies, waits for them, and re-layouts  60.9 us (12%)
  between operations  24.4 us (5%)
  matrix products  24.3 us (5%)
  starting transfers between devices  6.81 us (1%)
    psum x4, waiting for transfers between devices, spread(): return lax.psum(kept, axis)  212 us
    another operation x6, other arithmetic, on_device(): jax.scipy.linalg.solve_triangular(diag_block, rows, lower=True)  161 us
    another operation x53, local copies, waits for them, and re-layouts, on_device(): jax.scipy.linalg.solve_triangular(diag_block, rows, lower=True)  38.8 us
    all_to_all x1, waiting for transfers between devices, on_device(): lax.all_to_all(partial_value.reshape(slot_count * BLOCK, columns_all), 'r...  24.8 us
    another operation x28, matrix products, on_device(): jax.scipy.linalg.solve_triangular(diag_block, rows, lower=True)  16.7 us
  transfers between devices with their start and end apart: 5, of which 5 were waited for; matrix products, arithmetic and copies ran while one was open for 28% of the time, Pallas kernels for 0%

commit v1 on v0

--- a/solution.py
+++ b/solution.py
@@ -55,12 +55,20 @@
             (global_ids == k)[:, None, None], solution.astype(jnp.float32)[None], partial_value
         )
         solutions.append(solution)
-    stored = lax.all_to_all(
-        partial_value.reshape(slot_count * BLOCK, columns_all),
-        "row",
-        split_axis=1,
-        concat_axis=0,
-        tiled=True,
+    stored = jnp.concatenate(
+        lax.all_to_all(
+            jnp.stack(
+                jnp.split(
+                    partial_value.reshape(slot_count * BLOCK, columns_all),
+                    lax.axis_size("row"),
+                    axis=1,
+                )
+            ),
+            "row",
+            0,
+            0,
+        ),
+        axis=0,
     )
     ordered = jnp.take(stored.reshape(block_total, BLOCK, my_columns), block_home, axis=0)
     remainder = ordered.reshape(block_total * BLOCK, my_columns)

time: 521 us -> 554 us (1.063)
  local copies, waits for them, and re-layouts: 60.9 us -> 93.1 us
    another operation x0 -> x20, local copies, waits for them, and re-layouts: none -> 21.7 us  [the longest x18 21 us: on_device(): jnp.stack(jnp.split(partial_value.reshape(slot_count * BLOCK, columns_all...]
    unnamed x12 -> x31, local copies, waits for them, and re-layouts: 1.53 us -> 14.4 us
  transfers between devices with their start and end apart: 5 -> 5, of which waited for: 5 -> 5; matrix products, arithmetic and copies ran while one was open for 28% -> 27% of each run, Pallas kernels for 0% -> 0%
where the time goes in v1:
time: 554 us; the launch traced here: 551 us
  waiting for transfers between devices  237 us (43%)
  other arithmetic  166 us (30%)
  local copies, waits for them, and re-layouts  93.1 us (17%)
  between operations  24.4 us (4%)
  matrix products  24.3 us (4%)
  starting transfers between devices  6.81 us (1%)
    psum x4, waiting for transfers between devices, spread(): return lax.psum(kept, axis)  212 us
    another operation x6, other arithmetic, on_device(): jax.scipy.linalg.solve_triangular(diag_block, rows, lower=True)  161 us
    another operation x53, local copies, waits for them, and re-layouts, on_device(): jax.scipy.linalg.solve_triangular(diag_block, rows, lower=True)  39.5 us
    all_to_all x1, waiting for transfers between devices, on_device(): lax.all_to_all(jnp.stack(jnp.split(partial_value.reshape(slot_count * BLO...  24.8 us
    another operation x18, local copies, waits for them, and re-layouts, on_device(): jnp.stack(jnp.split(partial_value.reshape(slot_count * BLOCK, columns_all...  21 us
    another operation x28, matrix products, on_device(): jax.scipy.linalg.solve_triangular(diag_block, rows, lower=True)  16.7 us
    unnamed x31, local copies, waits for them, and re-layouts  14.4 us
  transfers between devices with their start and end apart: 5, of which 5 were waited for; matrix products, arithmetic and copies ran while one was open for 27% of the time, Pallas kernels for 0%

profile of v1, /device:TPU:9, one launch (start us, length us, event | category | flops | bytes accessed | tf_op | source)
XLA Modules:
  0.0 551.5 jit_solution(8728922168695491836)
XLA Ops:
  7.2 1.4 fusion.108
  17.6 4.5 dynamic-slice_bitcast_fusion.3
  22.1 2.0 fusion.19
  24.1 11.9 %while.8 = (s32[]{:T(128)}, f32[512,512]{1,0:T(8,128)}, s32[4,2]{0,1:T(2,128)S(1)}, f32[4,128,128]{2,1,0:T(8,128)S(1)}, s32[]{:T(128)}) while((s32[]{:T(128)}, f32[512,512]{1,0:T(8,128)}, s32[4,2]{0,1:T(2,128)S(1)}, f32[4,128,128]{2,1,0:T(8,128)S(1)}, s32[]{:T(128)}) %tuple.101), condition=%wide.while_cond, body=%wide.while_body.sunk | while | flops 2 | bytes 131181 | solution.py:42
  24.8 2.3 bitcast_dynamic-update-slice_fusion.8
  27.8 2.3 bitcast_dynamic-update-slice_fusion.8
  30.7 2.3 bitcast_dynamic-update-slice_fusion.8
  33.7 2.2 bitcast_dynamic-update-slice_fusion.8
  36.7 40.1 %custom-call.6 = f32[4,128,128]{1,2,0:T(8,128)S(1)} custom-call(f32[4,128,128]{2,1,0:T(8,128)} %copy-done.4), custom_call_target="InvertDiagBlocksLowerTriangular" | custom-call | tf_op jit(solution)/shard_map/jit(_solve_triangular)/triangular_solve | solution.py:42
  82.6 1.6 copy.87
  85.1 8.1 %while.9 = (s32[]{:T(128)}, f32[512,512]{1,0:T(8,128)S(1)}, s32[4,2]{0,1:T(2,128)S(1)}, f32[4,128,128]{2,1,0:T(8,128)S(1)}, s32[]{:T(128)}) while((s32[]{:T(128)}, f32[512,512]{1,0:T(8,128)S(1)}, s32[4,2]{0,1:T(2,128)S(1)}, f32[4,128,128]{2,1,0:T(8,128)S(1)}, s32[]{:T(128)}) %tuple.121), condition=%wide.while_cond.clone, body=%wide.while_body.clone.sunk | while | flops 2 | bytes 131181 | solution.py:42
  85.7 1.4 bitcast_dynamic-update-slice_fusion.9
  87.8 1.4 bitcast_dynamic-update-slice_fusion.9
  89.8 1.4 bitcast_dynamic-update-slice_fusion.9
  91.8 1.4 bitcast_dynamic-update-slice_fusion.9
  93.9 40.2 %custom-call.7 = f32[4,128,128]{1,2,0:T(8,128)S(1)} custom-call(f32[4,128,128]{2,1,0:T(8,128)} %copy-done.5), custom_call_target="InvertDiagBlocksLowerTriangular" | custom-call | tf_op jit(solution)/shard_map/jit(_solve_triangular)/triangular_solve | solution.py:42
  134.1 39.6 %all-reduce.5.cloned.1.call-done = bf16[512,256]{1,0:T(8,128)(2,1)} async-done(((bf16[512,256]{1,0:T(8,128)(2,1)}), bf16[512,256]{1,0:T(8,128)(2,1)}) %all-reduce.5.cloned.1.call-update) | async-done | bytes 262160 | tf_op jit(solution)/shard_map/psum | solution.py:13
  173.7 1.9 copy.85
  175.6 1.9 fusion.11
  183.8 11.7 %while.10 = (s32[]{:T(128)}, f32[512,512]{1,0:T(8,128)}, s32[4,2]{0,1:T(2,128)S(1)}, f32[4,128,128]{2,1,0:T(8,128)S(1)}, s32[]{:T(128)}) while((s32[]{:T(128)}, f32[512,512]{1,0:T(8,128)}, s32[4,2]{0,1:T(2,128)S(1)}, f32[4,128,128]{2,1,0:T(8,128)S(1)}, s32[]{:T(128)}) %tuple.122), condition=%wide.while_cond.clone.1, body=%wide.while_body.clone.1.sunk | while | flops 2 | bytes 131181 | solution.py:42
  184.4 2.3 bitcast_dynamic-update-slice_fusion.10
  187.4 2.3 bitcast_dynamic-update-slice_fusion.10
  190.3 2.3 bitcast_dynamic-update-slice_fusion.10
  193.3 2.2 bitcast_dynamic-update-slice_fusion.10
  196.0 39.3 %custom-call.8 = f32[4,128,128]{1,2,0:T(8,128)S(1)} custom-call(f32[4,128,128]{2,1,0:T(8,128)S(1)} %get-tuple-element.31), custom_call_target="InvertDiagBlocksLowerTriangular" | custom-call | tf_op jit(solution)/shard_map/jit(_solve_triangular)/triangular_solve | solution.py:42
  235.4 39.2 %all-reduce.7.cloned.1.call-done = bf16[512,256]{1,0:T(8,128)(2,1)} async-done(((bf16[512,256]{1,0:T(8,128)(2,1)}), bf16[512,256]{1,0:T(8,128)(2,1)}) %all-reduce.7.cloned.1.call-update) | async-done | bytes 262160 | tf_op jit(solution)/shard_map/psum | solution.py:13
  274.5 1.9 copy.89
  276.4 1.9 fusion.8
  284.3 8.1 %while.11 = (s32[]{:T(128)}, f32[512,512]{1,0:T(8,128)S(1)}, s32[4,2]{0,1:T(2,128)S(1)}, f32[4,128,128]{2,1,0:T(8,128)S(1)}, s32[]{:T(128)}) while((s32[]{:T(128)}, f32[512,512]{1,0:T(8,128)S(1)}, s32[4,2]{0,1:T(2,128)S(1)}, f32[4,128,128]{2,1,0:T(8,128)S(1)}, s32[]{:T(128)}) %tuple.123), condition=%wide.while_cond.clone.2, body=%wide.while_body.clone.2.sunk | while | flops 2 | bytes 131181 | solution.py:42
  285.0 1.3 bitcast_dynamic-update-slice_fusion.11
  287.0 1.3 bitcast_dynamic-update-slice_fusion.11
  293.1 39.3 %custom-call.9 = f32[4,128,128]{1,2,0:T(8,128)S(1)} custom-call(f32[4,128,128]{2,1,0:T(8,128)S(1)} %get-tuple-element.32), custom_call_target="InvertDiagBlocksLowerTriangular" | custom-call | tf_op jit(solution)/shard_map/jit(_solve_triangular)/triangular_solve | solution.py:42
  332.4 42.6 %all-reduce.9.cloned.1.call-done = bf16[512,256]{1,0:T(8,128)(2,1)} async-done(((bf16[512,256]{1,0:T(8,128)(2,1)}), bf16[512,256]{1,0:T(8,128)(2,1)}) %all-reduce.9.cloned.1.call-update) | async-done | bytes 262160 | tf_op jit(solution)/shard_map/psum | solution.py:13
  375.1 1.9 copy.92
  376.9 1.9 fusion.5
  382.1 90.4 %all-reduce.11.cloned.1.call-done = bf16[512,256]{1,0:T(8,128)(2,1)} async-done(((bf16[512,256]{1,0:T(8,128)(2,1)}), bf16[512,256]{1,0:T(8,128)(2,1)}) %all-reduce.11.cloned.1.call-update) | async-done | bytes 262160 | tf_op jit(solution)/shard_map/psum | solution.py:13
  473.6 1.8 fusion.2
  475.8 4.6 slice_bitcast_fusion
  482.3 1.8 copy.99
  484.1 1.8 copy.100
  486.0 1.8 copy.101
  487.8 1.8 copy.102
  496.8 1.5 constant_dynamic-update-slice_fusion.14
  498.3 1.5 constant_dynamic-update-slice_fusion.13
  499.7 1.5 constant_dynamic-update-slice_fusion.12
  501.2 1.5 constant_dynamic-update-slice_fusion.11
  509.7 6.5 %all-to-all-start = ((f32[16,1024,16]{1,2,0:T(8,128)}), f32[16,1024,16]{1,2,0:T(8,128)S(1)}, u32[]{:S(2)}, u32[]{:S(2)}) async-start(f32[16,1024,16]{1,2,0:T(8,128)} %constant_dynamic-update-slice_fusion), calls=%async_computation | async-start | bytes 2097152 | tf_op jit(solution)/shard_map/all_to_all | solution.py:59
  516.3 24.8 %all-to-all-done = f32[16,1024,16]{1,2,0:T(8,128)S(1)} async-done(((f32[16,1024,16]{1,2,0:T(8,128)}), f32[16,1024,16]{1,2,0:T(8,128)S(1)}, u32[]{:S(2)}, u32[]{:S(2)}) %all-to-all-start) | async-done | bytes 1048608 | tf_op jit(solution)/shard_map/all_to_all | solution.py:59
  (145 shorter events, 57.9 us)
Async XLA Ops:
  7.2 166.6 %all-reduce.5.cloned.1.call-start = ((), (), s32[]{:S(2)}) async-start(), calls=%async_computation.1 | async-start | bytes 524288 | tf_op jit(solution)/shard_map/psum | solution.py:13
  22.1 54.8 %copy-start.1 = (f32[1024,256]{1,0:T(8,128)S(1)}, f32[1024,256]{1,0:T(8,128)}, u32[]{:S(2)}) copy-start(f32[1024,256]{1,0:T(8,128)} %param.8) | copy-start | bytes 3145732
  24.1 60.8 %copy-start.6 = (s32[32]{0:T(128)S(1)}, s32[32]{0:T(128)}, u32[]{:S(2)}) copy-start(s32[32]{0:T(128)} %param.9) | copy-start | bytes 388
  36.0 0.7 copy-start.4
  82.6 191.9 %all-reduce.7.cloned.1.call-start = ((), (), s32[]{:S(2)}) async-start(), calls=%async_computation.2 | async-start | bytes 524288 | tf_op jit(solution)/shard_map/psum | solution.py:13
  93.2 0.7 copy-start.5
  93.9 81.7 %copy-start = (f32[512,512]{1,0:T(8,128)}, f32[512,512]{1,0:T(8,128)S(1)}, u32[]{:S(2)}) copy-start(f32[512,512]{1,0:T(8,128)S(1)} %get-tuple-element.296) | copy-start | bytes 3145732
  183.5 191.5 %all-reduce.9.cloned.1.call-start = ((), (), s32[]{:S(2)}) async-start(), calls=%async_computation.3 | async-start | bytes 524288 | tf_op jit(solution)/shard_map/psum | solution.py:13
  284.2 188.3 %all-reduce.11.cloned.1.call-start = ((), (), s32[]{:S(2)}) async-start(), calls=%async_computation.4 | async-start | bytes 524288 | tf_op jit(solution)/shard_map/psum | solution.py:13
  480.4 15.4 %copy-start.3 = (f32[1,1024,16]{2,1,0:T(8,128)S(1)}, f32[1,1024,16]{2,1,0:T(8,128)}, u32[]{:S(2)}) copy-start(f32[1,1024,16]{2,1,0:T(8,128)} %get-tuple-element.82) | copy-start | bytes 196612
  480.4 15.5 %copy-start.2 = (f32[1,1024,16]{2,1,0:T(8,128)S(1)}, f32[1,1024,16]{2,1,0:T(8,128)}, u32[]{:S(2)}) copy-start(f32[1,1024,16]{2,1,0:T(8,128)} %get-tuple-element.81) | copy-start | bytes 196612
  509.7 31.4 %all-to-all-start = ((f32[16,1024,16]{1,2,0:T(8,128)}), f32[16,1024,16]{1,2,0:T(8,128)S(1)}, u32[]{:S(2)}, u32[]{:S(2)}) async-start(f32[16,1024,16]{1,2,0:T(8,128)} %constant_dynamic-update-slice_fusion), calls=%async_computation | async-start | bytes 2097152 | tf_op jit(solution)/shard_map/all_to_all | solution.py:59
Sparse Core Ops, SparseCore 0:
  82.7 90.9 all-reduce.4
  183.6 90.8 all-reduce.6
  284.4 90.6 all-reduce.8
  382.2 90.2 all-reduce.10
